TPU v7x, 32 devices: a whole 2x2x4 slice. The times are simulated.
32 devices in a mesh: grp: 2 (over y), head: 16 (over z, x, core).
Axes of the slice: x: 2, y: 2, z: 4, core: 2. Of those that a mesh axis runs over, the one named last changes fastest.
Arguments:
- queries: bfloat16 [32, 16, 576], P('grp', 'head'), parts along dimension 0, may hold values from -32 to 32
- kv_pages: bfloat16 [16384, 64, 576], P(('grp', 'head')), parts along dimension 0, may hold values from -8 to 8
- page_table: int32 [32, 512], P('grp'), parts along dimension 0, may hold values from 0 to 8191, as said below
- lengths: int32 [32], P('grp'), parts along dimension 0, may hold values from 2048 to 32768
- selected: int32 [32, 32], P('grp'), parts along dimension 0, may hold values from 0 to 511, as said below
Outputs:
- attended: bfloat16 [32, 16, 512], P('grp', 'head'), parts along dimension 0
There are 2 independent parts, one for each index of `grp`. A program takes and returns all parts, laid end to end along the dimension named above; each array names one. Nothing has to cross between parts.
Inputs may be any that keep to these rules, and one draw needn't show every extreme that they name: `page_table`: every block of every request names a different page of the pool; the pages named by selected blocks fall at most 96 into one aligned run of 512 pages (one device's share of the pool), and some run holds exactly 96 of them. `selected`: each row names 32 different blocks of its request below ceil(lengths / 64); the first is the last such block.
All inputs are finite; a program needn't handle non-finite values.
Results may differ from a plain program's by a relative error of at most 0.0034.
Values may be sent and summed in bfloat16 or wider, within the bound.
No kernel may reach another device: no remote copies, remote signals or barrier semaphores. Data moves between devices by JAX's collectives and lax.ppermute only.
A program may use at most 128 MiB of HBM per device.

v0:
```python
import math

import jax
import jax.numpy as jnp
from jax import lax
from jax.sharding import PartitionSpec as P

ROPE = 64


SOFTMAX_SCALE = (0.1 * math.log(40.0) + 1.0) ** 2 / math.sqrt(192.0)


def local(queries, kv_pages, page_table, lengths, selected):
    channels = queries.shape[2]
    latent = channels - ROPE
    requests, pick_count = selected.shape
    pages_dev, page_len = (kv_pages.shape[0], kv_pages.shape[1])
    devices = lax.axis_size("head")
    capacity = 3 * requests * pick_count // devices
    own_index = lax.axis_index("head")
    all_queries = lax.all_gather(queries, "head", axis=1, tiled=True)
    page_ids = jnp.take_along_axis(page_table, selected, axis=1).reshape(-1)
    mine_mask = page_ids // pages_dev == own_index
    pair_count = requests * pick_count
    order_key = jnp.where(mine_mask, 0, pair_count) + jnp.arange(pair_count, dtype=jnp.int32)
    slot_ids = jnp.argsort(order_key)[:capacity]
    slot_live = mine_mask[slot_ids]
    slot_request = slot_ids // pick_count
    slot_block = selected.reshape(-1)[slot_ids]
    local_page = jnp.where(slot_live, page_ids[slot_ids] - own_index * pages_dev, 0)
    blocks = kv_pages[local_page]
    positions = slot_block[:, None] * page_len + jnp.arange(page_len, dtype=jnp.int32)[None, :]
    live_mask = slot_live[:, None] & (positions < lengths[slot_request][:, None])
    slot_queries = all_queries[slot_request]
    scores = (
        jnp.einsum("chd,ctd->cht", slot_queries, blocks, preferred_element_type=jnp.float32)
        * SOFTMAX_SCALE
    )
    masked = jnp.where(live_mask[:, None, :], scores, jnp.float32(-1e30))
    slot_top = jnp.max(masked, axis=2)
    owner_mask = slot_request[:, None] == jnp.arange(requests, dtype=jnp.int32)[None, :]
    local_top = jnp.max(
        jnp.where(owner_mask[:, :, None], slot_top[:, None, :], jnp.float32(-1e30)), axis=0
    )
    row_top = lax.pmax(local_top, "head")
    weights = jnp.where(
        live_mask[:, None, :], jnp.exp(masked - row_top[slot_request][:, :, None]), jnp.float32(0.0)
    )
    onehot = owner_mask.astype(jnp.float32)
    totals = jnp.einsum(
        "cr,ch->rh", onehot, jnp.sum(weights, axis=2), precision=lax.Precision.HIGHEST
    )
    slot_numer = jnp.einsum(
        "cht,cte->che",
        weights.astype(jnp.bfloat16),
        blocks[:, :, :latent],
        preferred_element_type=jnp.float32,
    )
    numer_sum = jnp.einsum("cr,che->rhe", onehot, slot_numer, precision=lax.Precision.HIGHEST)
    numer_own, totals_own = (
        lax.psum_scatter(numer_sum, "head", scatter_dimension=1, tiled=True),
        lax.psum_scatter(totals, "head", scatter_dimension=1, tiled=True),
    )
    return (numer_own / totals_own[:, :, None]).astype(jnp.bfloat16)


def solution(mesh):
    return jax.shard_map(
        local,
        mesh=mesh,
        in_specs=(
            P("grp", "head", None),
            P(("grp", "head"), None, None),
            P("grp", None),
            P("grp"),
            P("grp", None),
        ),
        out_specs=P("grp", "head", None),
        check_vma=False,
    )
```

profile of v0, /device:TPU:0, one launch (start us, length us, event | category | flops | bytes accessed | tf_op | source)
XLA Modules:
  0.0 230.4 jit_solution(13203962640777853632)
XLA Ops:
  6.5 0.0 copy-start
  6.5 0.0 copy-start.2
  6.5 0.0 reduce-scatter.2.cloned.1.call-start
  6.5 0.8 bitcast_or_fusion
  7.3 0.8 reshape.115
  8.1 1.9 fusion.22
  10.0 0.1 reshape.187
  10.1 0.0 copy-done
  10.1 4.5 %gather_fusion.6 = s32[512]{0:T(512)S(1)} fusion(s32[16,512]{1,0:T(8,128)S(1)} %copy-done, s32[512]{0:T(512)S(1)} %reshape.187), kind=kCustom, calls=%fused_computation.6 | custom fusion | bytes 8192 | tf_op jit(solution)/shard_map/jit(take_along_axis)/gather | solution.py:23
  14.6 0.1 reshape.190
  14.7 0.0 copy-done.2
  14.7 0.1 select_n.73
  14.8 3.8 %sort.17 = (s32[512]{0:T(512)}, s32[512]{0:T(512)S(1)}) sort(s32[512]{0:T(512)S(1)} %get-tuple-element.9, s32[512]{0:T(512)S(1)} %iota.23), dimensions={0}, to_apply=%region_0.0 | sort | flops 4608 | bytes 8192 | tf_op jit(solution)/shard_map/jit(argsort)/sort | solution.py:27
  18.6 9.9 %compare_select_fusion.3 = (s32[96]{0:T(128)S(1)}, s32[96]{0:T(128)S(1)}, s32[96]{0:T(128)S(1)}) fusion(s32[]{:T(128)} %bitcast.2, s32[]{:T(128)} %bitcast.3, s32[]{:T(128)} %bitcast.4, s32[]{:T(128)} %bitcast.5, s32[]{:T(128)} %bitcast.6, s32[]{:T(128)} %bitcast.7, s32[]{:T(128)} %bitcast.8, s32[]{:T(128)} %bitcast.9, s32[]{:T(128)} %bitcast.10, ...), kind=kLoop, calls=%fused_computation.45 | loop fusion | flops 4800 | bytes 1600 | tf_op jit(solution)/shard_map/gather | solution.py:34
  28.6 1.3 gather_fusion.3
  29.8 1.2 gather_fusion
  31.1 0.0 copy-start.3
  31.1 55.1 %copy.20 = bf16[512,64,576]{2,1,0:T(8,128)(2,1)} copy(bf16[512,64,576]{0,2,1:T(8,128)(2,1)} %param.6) | data formatting | bytes 75497472 | tf_op args[1]
  86.2 0.0 copy-done.3
  86.2 24.0 %all_gather.3 = bf16[16,16,576]{2,0,1:T(8,128)(2,1)S(1)} all-gather(bf16[16,1,576]{2,0,1:T(8,128)(2,1)S(1)} %copy-done.3), channel_id=1, replica_groups=mesh['grp'=2,'head'=16] {'head'}, dimensions={1}, use_global_device_ids=true | all-gather | bytes 313344 | tf_op jit(solution)/shard_map/all_gather | solution.py:22
  110.2 0.1 copy.19
  110.3 1.3 gather_fusion.1
  111.6 12.2 %gather_fusion.4 = bf16[96,64,576]{2,1,0:T(8,128)(2,1)} fusion(bf16[512,64,576]{2,1,0:T(8,128)(2,1)} %copy.20, s32[1024]{0:T(1024)S(1)} %pad_clamp_fusion), kind=kCustom, calls=%fused_computation.4 | custom fusion | bytes 14156160 | tf_op jit(solution)/shard_map/gather | solution.py:32
  123.8 0.9 gather_fusion.2
  124.7 0.1 fusion.11
  124.8 4.9 %fusion.23 = (f32[96,16]{1,0:T(8,128)S(1)}, f32[96,16,64]{2,1,0:T(8,128)S(1)}) fusion(bf16[96,16,576]{2,1,0:T(8,128)(2,1)S(1)} %gather_fusion.2, bf16[96,64,576]{2,1,0:T(8,128)(2,1)} %gather_fusion.4, pred[96,64]{1,0:T(8,128)(4,1)S(1)} %fusion.11), kind=kOutput, calls=%fused_computation.70 | convolution fusion | flops 113539584 | bytes 9252864 | tf_op jit(solution)/shard_map/chd,ctd->cht/dot_general | solution.py:37
  129.8 0.1 copy.21
  129.9 0.1 select_reduce_fusion
  130.0 30.0 %pmax.7 = f32[16,16]{1,0:T(8,128)S(1)} all-reduce(f32[16,16]{1,0:T(8,128)S(1)} %select_reduce_fusion), channel_id=1, replica_groups=mesh['grp'=2,'head'=16] {'head'}, use_global_device_ids=true, to_apply=%region_3.4 | all-reduce | flops 256 | bytes 2048 | tf_op jit(solution)/shard_map/pmax | solution.py:46
  160.0 0.6 gather_fusion.5
  160.6 0.0 copy-start.1
  160.6 0.0 copy-start.4
  160.6 3.8 %fusion = f32[96,16,512]{2,1,0:T(8,128)S(1)} fusion(bf16[96,64,576]{2,1,0:T(8,128)(2,1)} %gather_fusion.4, f32[96,16,64]{2,1,0:T(8,128)S(1)} %get-tuple-element.29, f32[96,16]{1,0:T(8,128)S(1)} %gather_fusion.5, pred[96,64]{1,0:T(8,128)(4,1)S(1)} %fusion.11), kind=kOutput, calls=%fused_computation.7 | convolution fusion | flops 100958208 | bytes 9842688 | tf_op jit(solution)/shard_map/cht,cte->che/dot_general | solution.py:54
  164.5 3.7 %fusion.2 = f32[16,16,512]{2,0,1:T(8,128)} fusion(f32[96,16,512]{2,1,0:T(8,128)S(1)} %fusion, s32[96]{0:T(128)S(1)} %get-tuple-element.8), kind=kOutput, calls=%fused_computation.9 | convolution fusion | flops 150996480 | bytes 3670400 | tf_op jit(solution)/shard_map/cr,che->rhe/dot_general | solution.py:60
  168.1 0.0 reduce-scatter.2.cloned.1.call-update
  168.2 0.0 copy-done.4
  168.2 0.6 dynamic-slice
  168.8 0.5 fusion.5
  169.3 0.2 fusion.13
  169.5 30.1 %all-reduce = f32[16,16]{0,1:T(8,128)S(1)} all-reduce(f32[16,16]{0,1:T(8,128)S(1)} %fusion.13), channel_id=3, replica_groups=mesh['grp'=2,'head'=16] {'head'}, use_global_device_ids=true, to_apply=%region_6.7.clone | all-reduce | flops 256 | bytes 2048
  199.6 0.7 dynamic-slice_bitcast_fusion
  200.3 21.8 %reduce-scatter.2.cloned.1.call-done = f32[16,1,512]{2,0,1:T(8,128)} async-done(((f32[16,16,512]{2,0,1:T(8,128)}), f32[16,1,512]{2,0,1:T(8,128)}) %reduce-scatter.2.cloned.1.call-update) | async-done | bytes 32784 | tf_op jit(solution)/shard_map/reduce_scatter | solution.py:62
  222.1 1.4 divide_convert_fusion
  223.5 0.0 copy-done.1
  (10 shorter events, 0.1 us)
Async XLA Ops:
  6.5 3.6 %copy-start = (s32[16,512]{1,0:T(8,128)S(1)}, s32[16,512]{1,0:T(8,128)}, u32[]{:S(2)}) copy-start(s32[16,512]{1,0:T(8,128)} %param.7) | copy-start | bytes 98308
  6.5 8.2 %copy-start.2 = (s32[16,32]{1,0:T(8,128)S(1)}, s32[16,32]{1,0:T(8,128)}, u32[]{:S(2)}) copy-start(s32[16,32]{1,0:T(8,128)} %param.9) | copy-start | bytes 6148
  6.5 215.6 %reduce-scatter.2.cloned.1.call-start = ((), (), s32[]{:S(2)}) async-start(), calls=%async_computation.1 | async-start | bytes 557056 | tf_op jit(solution)/shard_map/reduce_scatter | solution.py:62
  31.1 55.1 %copy-start.3 = (bf16[16,1,576]{2,0,1:T(8,128)(2,1)S(1)}, bf16[16,1,576]{2,0,1:T(8,128)(2,1)}, u32[]{:S(2)}) copy-start(bf16[16,1,576]{2,0,1:T(8,128)(2,1)} %param.5) | copy-start | bytes 55300
  160.6 62.9 %copy-start.1 = (s32[16,512]{1,0:T(8,128)S(1)}, s32[16,512]{1,0:T(8,128)}, u32[]{:S(2)}) copy-start(s32[16,512]{1,0:T(8,128)} %param.7) | copy-start | bytes 98308
  160.6 7.5 %copy-start.4 = (u32[32]{0:T(128)S(1)}, u32[32]{0:T(128)}, u32[]{:S(2)}) copy-start(u32[32]{0:T(128)} %constant.94) | copy-start | bytes 388
Sparse Core Ops, SparseCore 0:
  168.3 53.7 reduce-scatter.1
where the time goes:
time: 232 us; the launch traced here: 230 us
  blocking collectives  84.1 us (36%)
  local copies, waits for them, and re-layouts  81.5 us (35%)
  waiting for transfers between devices  21.9 us (9%)
  other arithmetic  16.7 us (7%)
  between operations  13.6 us (6%)
  matrix products  12.6 us (5%)
    unnamed x12, local copies, waits for them, and re-layouts  55.7 us
    unnamed x1, blocking collectives  30.1 us
    pmax x1, blocking collectives, local(): row_top = lax.pmax(local_top, 'head')  30 us
    all_gather x1, blocking collectives, local(): all_queries = lax.all_gather(queries, 'head', axis=1, tiled=True)  24 us
    reduce_scatter x1, waiting for transfers between devices, local(): lax.psum_scatter(numer_sum, 'head', scatter_dimension=1, tiled=True)  21.8 us
    gather x1, local copies, waits for them, and re-layouts, local(): blocks = kv_pages[local_page]  12.2 us
    gather x1, other arithmetic, local(): lengths[slot_request][:, None]  9.93 us
    dot_general x1, matrix products, local(): jnp.einsum('chd,ctd->cht', slot_queries, blocks, preferred_element_type=j...  4.93 us
  transfers between devices with their start and end apart: 1, of which 1 were waited for; matrix products, arithmetic and copies ran while one was open for 1% of the time, Pallas kernels for 0%

commit v1 on v0

v1 whole, which is shorter than its diff:
```python
import functools
import math

import jax
import jax.numpy as jnp
from jax import lax
from jax.experimental import pallas as pl
from jax.experimental.pallas import tpu as pltpu
from jax.sharding import PartitionSpec as P

ROPE = 64
LANES = 128
NEG = -1e30

SOFTMAX_SCALE = (0.1 * math.log(40.0) + 1.0) ** 2 / math.sqrt(192.0)


def attend_kernel(
    sizes, lengths_ref, table_ref, picks_ref, queries_ref, pool_ref, out_ref,
    pages, scores, tops, numer, sems,
):
    reqs, heads, latent, chunk = sizes
    tiles, tokens, channels, width = pages.shape
    picks, blocks = picks_ref.shape[0], table_ref.shape[1]
    pool = pool_ref.shape[2]
    chunks = tokens // chunk
    first_page = lax.axis_index("head") * pool

    block_lane = lax.broadcasted_iota(jnp.int32, (picks, blocks), 1)
    pool_lane = lax.broadcasted_iota(jnp.int32, (picks, pool), 1)
    owner_all = jnp.zeros((picks, pool), jnp.float32)
    count_all = jnp.zeros((picks, pool), jnp.float32)
    for r in range(reqs):
        pick = picks_ref[:, r : r + 1]
        row = table_ref[r : r + 1, :].astype(jnp.float32)
        page = jnp.sum(
            jnp.where(block_lane == pick, row, 0.0), axis=1, keepdims=True
        ).astype(jnp.int32)
        count = jnp.clip(lengths_ref[r] - pick * tokens, 0, tokens)
        hit = pool_lane == page - first_page
        owner_all = jnp.where(hit, float(r + 1), owner_all)
        count_all = jnp.where(hit, count.astype(jnp.float32), count_all)
    owner = jnp.sum(owner_all, axis=0, keepdims=True)
    count = jnp.sum(count_all, axis=0, keepdims=True).astype(jnp.int32)

    def lanes(x, tile):
        return x[:, tile * width : (tile + 1) * width]

    needed = [jnp.max(lanes(owner, tile)) > 0.5 for tile in range(tiles)]
    owner = owner.astype(jnp.int32) - 1

    def fetch(tile, part):
        return pltpu.make_async_copy(
            pool_ref.at[pl.ds(part * chunk, chunk), :, pl.ds(tile * width, width)],
            pages.at[tile, pl.ds(part * chunk, chunk)],
            sems.at[tile, part],
        )

    for tile in range(tiles):
        @pl.when(needed[tile])
        def _(tile=tile):
            for part in range(chunks):
                fetch(tile, part).start()

    tops[...] = jnp.full(tops.shape, NEG, jnp.float32)
    numer[...] = jnp.zeros(numer.shape, jnp.float32)
    group = 2 if width == LANES else 1

    for tile in range(tiles):
        @pl.when(needed[tile])
        def _(tile=tile):
            own = lanes(owner, tile)
            live = lanes(count, tile)
            own_wide = jnp.concatenate([own] * group, axis=1)

            @pl.loop(0, chunks)
            def _(part):
                fetch(tile, part).wait()
                top = tops[tile]
                for t in range(0, chunk, group):
                    token = part * chunk + t
                    keys = [pages[tile, token + g] for g in range(group)]
                    both = jnp.dot(
                        queries_ref[...],
                        jnp.concatenate(keys, axis=1),
                        preferred_element_type=jnp.float32,
                    )
                    mine = both[:heads]
                    for r in range(1, reqs):
                        mine = jnp.where(own_wide == r, both[r * heads : (r + 1) * heads], mine)
                    for g in range(group):
                        score = mine[:, g * width : (g + 1) * width] * SOFTMAX_SCALE
                        score = jnp.where(live > token + g, score, NEG)
                        scores[tile, token + g] = score
                        top = jnp.maximum(top, score)
                tops[tile] = top

    row_top = []
    for r in range(reqs):
        best = jnp.full((heads, width), NEG, jnp.float32)
        for tile in range(tiles):
            best = jnp.maximum(best, jnp.where(lanes(owner, tile) == r, tops[tile], NEG))
        row_top.append(jnp.max(best, axis=1, keepdims=True))

    total = [jnp.zeros((heads, width), jnp.float32) for _ in range(reqs)]
    sums = tops
    for tile in range(tiles):
        own = lanes(owner, tile)
        shift = jnp.zeros((heads, width), jnp.float32)
        for r in range(reqs):
            shift = jnp.where(own == r, row_top[r], shift)
        sums[tile] = jnp.zeros((heads, width), jnp.float32)

        @pl.when(needed[tile])
        def _(tile=tile, own=own, shift=shift):
            live = lanes(count, tile)

            @pl.loop(0, chunks)
            def _(part):
                acc = sums[tile]
                weights, values = [], []
                for t in range(chunk):
                    token = part * chunk + t
                    weight = jnp.where(live > token, jnp.exp(scores[tile, token] - shift), 0.0)
                    acc = acc + weight
                    spread = [jnp.where(own == r, weight, 0.0).astype(jnp.bfloat16) for r in range(reqs)]
                    weights.append(jnp.concatenate(spread, axis=0))
                    values.append(pages[tile, token, :latent])
                sums[tile] = acc
                numer[...] += lax.dot_general(
                    jnp.concatenate(weights, axis=1),
                    jnp.concatenate(values, axis=1),
                    (((1,), (1,)), ((), ())),
                    preferred_element_type=jnp.float32,
                )

    tail = lax.broadcasted_iota(jnp.int32, (heads, LANES), 1)
    for r in range(reqs):
        total = jnp.zeros((heads, width), jnp.float32)
        for tile in range(tiles):
            total = total + jnp.where(lanes(owner, tile) == r, sums[tile], 0.0)
        total = jnp.sum(total, axis=1, keepdims=True)
        out_ref[r, :, :latent] = numer[r * heads : (r + 1) * heads]
        out_ref[r, :, latent:] = jnp.where(tail == 0, row_top[r], jnp.where(tail == 1, total, 0.0))


def attend(queries, pool, page_table, lengths, selected):
    reqs, heads, channels = queries.shape
    tokens, _, pages_dev = pool.shape
    latent = channels - ROPE
    width = LANES if pages_dev % LANES == 0 else pages_dev
    tiles = pages_dev // width
    chunk = math.gcd(8, tokens)
    rows = reqs * heads
    vmem = pl.BlockSpec(memory_space=pltpu.VMEM)
    return pl.pallas_call(
        functools.partial(attend_kernel, (reqs, heads, latent, chunk)),
        out_shape=jax.ShapeDtypeStruct((reqs, heads, latent + LANES), jnp.float32),
        in_specs=[
            pl.BlockSpec(memory_space=pltpu.SMEM), vmem, vmem, vmem,
            pl.BlockSpec(memory_space=pl.ANY),
        ],
        out_specs=vmem,
        scratch_shapes=[
            pltpu.VMEM((tiles, tokens, channels, width), jnp.bfloat16),
            pltpu.VMEM((tiles, tokens, heads, width), jnp.float32),
            pltpu.VMEM((tiles, heads, width), jnp.float32),
            pltpu.VMEM((rows, latent), jnp.float32),
            pltpu.SemaphoreType.DMA((tiles, tokens // chunk)),
        ],
        compiler_params=pltpu.CompilerParams(vmem_limit_bytes=58 * 2**20),
        name="attend",
    )(lengths, page_table, selected.T, queries.reshape(rows, channels), pool)


def merge(mine, theirs, latent):
    top_lane = lax.broadcasted_iota(jnp.int32, mine.shape, 2) == latent
    mine_top, their_top = mine[:, :, latent : latent + 1], theirs[:, :, latent : latent + 1]
    top = jnp.maximum(mine_top, their_top)
    both = mine * jnp.exp(mine_top - top) + theirs * jnp.exp(their_top - top)
    return jnp.where(top_lane, top, both)


def local(queries, kv_pages, page_table, lengths, selected):
    latent = queries.shape[2] - ROPE
    devices = lax.axis_size("head")
    strides = [1 << b for b in reversed(range(devices.bit_length() - 1))]

    def swap(x, stride):
        return lax.ppermute(x, "head", [(i, i ^ stride) for i in range(devices)])

    gathered = queries.transpose(1, 0, 2)
    for stride in strides:
        gathered = jnp.concatenate([gathered, swap(gathered, stride)], axis=0)
    part = attend(
        gathered.transpose(1, 0, 2), kv_pages.transpose(1, 2, 0), page_table, lengths, selected
    ).transpose(1, 0, 2)
    for stride in reversed(strides):
        half = part.shape[0] // 2
        part = merge(part[:half], swap(part[half:], stride), latent)
    out = part[0, :, :latent] / part[0, :, latent + 1 : latent + 2]
    return out.astype(jnp.bfloat16)[:, None, :]


def solution(mesh):
    return jax.shard_map(
        local,
        mesh=mesh,
        in_specs=(
            P("grp", "head", None),
            P(("grp", "head"), None, None),
            P("grp", None),
            P("grp"),
            P("grp", None),
        ),
        out_specs=P("grp", "head", None),
        check_vma=False,
    )
```

time: 232 us -> 57.5 us (0.25)
  blocking collectives: 84.1 us -> 0 us
  local copies, waits for them, and re-layouts: 81.5 us -> 6.51 us
  starting transfers between devices: 0.01 us -> 14.8 us
  Pallas kernels: 0 us -> 13.8 us
  between operations: 13.6 us -> 0.15 us
  matrix products: 12.6 us -> 0 us
  other arithmetic: 16.7 us -> 5.01 us
  waiting for transfers between devices: 21.9 us -> 16.7 us
    unnamed x12 -> x5, local copies, waits for them, and re-layouts: 55.7 us -> 2.14 us
    unnamed x1 -> x0, blocking collectives: 30.1 us -> none
    pmax x1 -> x0, blocking collectives: 30 us -> none  [local(): row_top = lax.pmax(local_top, 'head')]
    gather x10 -> x0, local copies, waits for them, and re-layouts: 24.2 us -> none  [the longest x1 12.2 us: local(): blocks = kv_pages[local_page]]
    all_gather x1 -> x0, blocking collectives: 24 us -> none  [local(): all_queries = lax.all_gather(queries, 'head', axis=1, tiled=True)]
    reduce_scatter x1 -> x0, waiting for transfers between devices: 21.8 us -> none  [local(): lax.psum_scatter(numer_sum, 'head', scatter_dimension=1, tiled=True)]
    ppermute x0 -> x8, waiting for transfers between devices: none -> 16.7 us  [swap(): return lax.ppermute(x, 'head', [(i, i ^ stride) for i in range(devices)])]
    ppermute x0 -> x8, starting transfers between devices: none -> 14.8 us  [swap(): return lax.ppermute(x, 'head', [(i, i ^ stride) for i in range(devices)])]
  transfers between devices with their start and end apart: 1 -> 8, of which waited for: 1 -> 7; matrix products, arithmetic and copies ran while one was open for 1% -> 4% of each run, Pallas kernels for 0% -> 0%
where the time goes in v1:
time: 57.5 us; the launch traced here: 57 us
  waiting for transfers between devices  16.7 us (29%)
  starting transfers between devices  14.8 us (26%)
  Pallas kernels  13.8 us (24%)
  local copies, waits for them, and re-layouts  6.51 us (11%)
  other arithmetic  5.01 us (9%)
    ppermute x8, waiting for transfers between devices, swap(): return lax.ppermute(x, 'head', [(i, i ^ stride) for i in range(devices)])  16.7 us
    ppermute x8, starting transfers between devices, swap(): return lax.ppermute(x, 'head', [(i, i ^ stride) for i in range(devices)])  14.8 us
    pallas_call x1, Pallas kernels, attend(): pl.pallas_call(functools.partial(attend_kernel, (reqs, heads, latent, chu...  13.8 us
    concatenate x3, other arithmetic, local(): gathered = jnp.concatenate([gathered, swap(gathered, stride)], axis=0)  2.24 us
    unnamed x5, local copies, waits for them, and re-layouts  2.14 us
    select_n x4, other arithmetic, merge(): return jnp.where(top_lane, top, both)  1.47 us
  transfers between devices with their start and end apart: 8, of which 7 were waited for; matrix products, arithmetic and copies ran while one was open for 4% of the time, Pallas kernels for 0%

profile of v1, /device:TPU:0, one launch (start us, length us, event | category | flops | bytes accessed | tf_op | source)
XLA Modules:
  0.0 57.0 jit_solution(2601693678523701085)
XLA Ops:
  0.0 4.1 %collective-permute-start = (bf16[1,16,576]{2,1,0:T(8,128)(2,1)}, bf16[1,16,576]{2,1,0:T(8,128)(2,1)S(1)}, u32[]{:S(2)}, u32[]{:S(2)}) collective-permute-start(bf16[1,16,576]{2,1,0:T(8,128)(2,1)} %bitcast.31), channel_id=1, source_target_pairs={{0,8},{1,9},{2,10},{3,11},{4,12},{5,13},{6,14},{7,15},{8,0},{9,1},... | collective-permute-start | bytes 55304 | tf_op jit(solution)/shard_map/ppermute | solution.py:190
  4.1 2.0 %collective-permute-done = bf16[1,16,576]{2,1,0:T(8,128)(2,1)S(1)} collective-permute-done((bf16[1,16,576]{2,1,0:T(8,128)(2,1)}, bf16[1,16,576]{2,1,0:T(8,128)(2,1)S(1)}, u32[]{:S(2)}, u32[]{:S(2)}) %collective-permute-start) | collective-permute-done | bytes 18464 | tf_op jit(solution)/shard_map/ppermute | solution.py:190
  6.0 0.7 %pad_maximum_fusion.2 = bf16[2,16,576]{2,1,0:T(8,128)(2,1)S(1)} fusion(bf16[1,16,576]{2,1,0:T(8,128)(2,1)S(1)} %collective-permute-done, bf16[1,16,576]{2,1,0:T(8,128)(2,1)} %bitcast.32), kind=kLoop, calls=%fused_computation.17 | loop fusion | flops 18432 | bytes 73728 | tf_op jit(solution)/shard_map/concatenate | solution.py:194
  6.8 2.0 %collective-permute-start.1 = (bf16[2,16,576]{2,1,0:T(8,128)(2,1)S(1)}, bf16[2,16,576]{2,1,0:T(8,128)(2,1)S(1)}, u32[]{:S(2)}, u32[]{:S(2)}) collective-permute-start(bf16[2,16,576]{2,1,0:T(8,128)(2,1)S(1)} %pad_maximum_fusion.2), channel_id=1, source_target_pairs={{0,4},{1,5},{2,6},{3,7},{4,0},{5,1},{6,2},{7,3},{8,12},{9,13},{10,... | collective-permute-start | bytes 110600 | tf_op jit(solution)/shard_map/ppermute | solution.py:190
  8.8 0.7 %constant_dynamic-update-slice_fusion.4 = bf16[16,16,576]{2,1,0:T(8,128)(2,1)S(1)} fusion(bf16[16,1,576]{2,0,1:T(8,128)(2,1)} %param.5), kind=kLoop, calls=%fused_computation.31 | loop fusion | bytes 38912
  9.5 1.4 %copy.48 = s32[16,32]{0,1:T(8,128)} copy(s32[16,32]{1,0:T(8,128)} %param.9) | data formatting | bytes 4096 | tf_op args[4]
  10.9 0.0 collective-permute-done.1
  10.9 0.7 %pad_maximum_fusion.1 = bf16[4,16,576]{2,1,0:T(8,128)(2,1)S(1)} fusion(bf16[2,16,576]{2,1,0:T(8,128)(2,1)S(1)} %collective-permute-done.1, bf16[1,16,576]{2,1,0:T(8,128)(2,1)S(1)} %collective-permute-done, bf16[1,16,576]{2,1,0:T(8,128)(2,1)} %bitcast.33), kind=kLoop, calls=%fused_computation.10 | loop fusion | flops 73728 | bytes 147456 | tf_op jit(solution)/shard_map/concatenate | solution.py:194
  11.6 2.0 %collective-permute-start.2 = (bf16[4,16,576]{2,1,0:T(8,128)(2,1)S(1)}, bf16[4,16,576]{2,1,0:T(8,128)(2,1)S(1)}, u32[]{:S(2)}, u32[]{:S(2)}) collective-permute-start(bf16[4,16,576]{2,1,0:T(8,128)(2,1)S(1)} %pad_maximum_fusion.1), channel_id=1, source_target_pairs={{0,2},{1,3},{2,0},{3,1},{4,6},{5,7},{6,4},{7,5},{8,10},{9,11},{10,... | collective-permute-start | bytes 221192 | tf_op jit(solution)/shard_map/ppermute | solution.py:190
  13.6 2.5 %collective-permute-done.2 = bf16[4,16,576]{2,1,0:T(8,128)(2,1)S(1)} collective-permute-done((bf16[4,16,576]{2,1,0:T(8,128)(2,1)S(1)}, bf16[4,16,576]{2,1,0:T(8,128)(2,1)S(1)}, u32[]{:S(2)}, u32[]{:S(2)}) %collective-permute-start.2) | collective-permute-done | bytes 73760 | tf_op jit(solution)/shard_map/ppermute | solution.py:190
  16.1 0.8 %pad_maximum_fusion = bf16[8,16,576]{2,1,0:T(8,128)(2,1)S(1)} fusion(bf16[4,16,576]{2,1,0:T(8,128)(2,1)S(1)} %collective-permute-done.2, bf16[2,16,576]{2,1,0:T(8,128)(2,1)S(1)} %collective-permute-done.1, bf16[1,16,576]{2,1,0:T(8,128)(2,1)S(1)} %collective-permute-done, bf16[1,16,576]{2,1,0:T(8,128)(2,1)} %bitcast.34), kind=kLoop, calls=%fused_computation.6 | loop fusion | flops 221184 | bytes 294912 | tf_op jit(solution)/shard_map/concatenate | solution.py:194
  16.9 0.1 collective-permute-start.3
  17.0 1.3 %collective-permute-done.3 = bf16[8,16,576]{2,1,0:T(8,128)(2,1)S(1)} collective-permute-done((bf16[8,16,576]{2,1,0:T(8,128)(2,1)S(1)}, bf16[8,16,576]{2,1,0:T(8,128)(2,1)S(1)}, u32[]{:S(2)}, u32[]{:S(2)}) %collective-permute-start.3) | collective-permute-done | bytes 147488 | tf_op jit(solution)/shard_map/ppermute | solution.py:190
  18.4 0.8 %copy.49 = bf16[16,16,576]{2,1,0:T(8,128)(2,1)} copy(bf16[16,16,576]{2,0,1:T(8,128)(2,1)S(1)} %bitcast.30) | data formatting | bytes 589824 | tf_op jit(solution)/shard_map/transpose | solution.py:196
  19.1 13.8 %attend.1 = f32[16,16,640]{2,1,0:T(8,128)} custom-call(s32[16]{0:T(128)} %lengths_ref.1, s32[16,512]{1,0:T(8,128)} %table_ref.1, s32[32,16]{1,0:T(8,128)} %bitcast.35, bf16[256,576]{1,0:T(8,128)(2,1)} %bitcast.29, bf16[64,576,512]{2,1,0:T(8,128)(2,1)} %bitcast.25), custom_call_target="tpu_custom_call" | custom-call | tf_op jit(solution)/shard_map/attend/pallas_call | solution.py:156
  32.9 1.0 %slice.77 = f32[8,16,640]{2,0,1:T(8,128)S(1)} slice(f32[16,16,640]{2,0,1:T(8,128)} %bitcast.26), slice={[8:16], [0:16], [0:640]} | slice | bytes 655360 | tf_op jit(solution)/shard_map/slice | solution.py:200
  33.9 0.2 collective-permute-start.4
  34.1 1.5 %collective-permute-done.4 = f32[8,16,640]{2,0,1:T(8,128)S(1)} collective-permute-done((f32[8,16,640]{2,0,1:T(8,128)S(1)}, f32[8,16,640]{2,0,1:T(8,128)S(1)}, u32[]{:S(2)}, u32[]{:S(2)}) %collective-permute-start.4) | collective-permute-done | bytes 327712 | tf_op jit(solution)/shard_map/ppermute | solution.py:190
  35.6 0.9 %subtract_exponential_fusion.1 = (f32[8,16,1]{2,0,1:T(8,128)S(1)}, f32[8,16,1]{2,0,1:T(8,128)S(1)}) fusion(f32[16,16,640]{2,0,1:T(8,128)} %bitcast.27, f32[8,16,640]{2,0,1:T(8,128)S(1)} %collective-permute-done.4), kind=kLoop, calls=%fused_computation.13 | loop fusion | flops 256 | bytes 2048 | tf_op jit(solution)/shard_map/exp | solution.py:180
  36.5 0.2 copy.70
  36.6 0.2 copy.69
  36.8 0.2 copy.71
  37.0 1.1 %fusion.1 = f32[8,16,640]{2,0,1:T(8,128)S(1)} fusion(f32[16,16,640]{2,0,1:T(8,128)} %bitcast.28, f32[8,16,640]{2,0,1:T(8,128)S(1)} %collective-permute-done.4, f32[8,16]{0,1:T(8,128)S(1)} %bitcast.38, f32[8,16]{0,1:T(8,128)S(1)} %bitcast.36, f32[8,16]{0,1:T(8,128)S(1)} %bitcast.37, pred[640]{0:T(1024)(128)(4,1)S(1)} %iota_compare_fusion), kind=kLoop, calls=%fused_computation.2 | loop fusion | flops 327680 | bytes 985216 | tf_op jit(solution)/shard_map/jit(_where)/select_n | solution.py:181
  38.1 2.0 %collective-permute-start.5 = (f32[4,16,640]{2,0,1:T(4,128)S(1)}, f32[4,16,640]{2,0,1:T(4,128)S(1)}, u32[]{:S(2)}, u32[]{:S(2)}) collective-permute-start(f32[4,16,640]{2,0,1:T(4,128)S(1)} %slice.81), channel_id=1, source_target_pairs={{0,2},{1,3},{2,0},{3,1},{4,6},{5,7},{6,4},{7,5},{8,10},{9,11},{10,... | collective-permute-start | bytes 491528 | tf_op jit(solution)/shard_map/ppermute | solution.py:190
  40.1 4.5 %collective-permute-done.5 = f32[4,16,640]{2,0,1:T(4,128)S(1)} collective-permute-done((f32[4,16,640]{2,0,1:T(4,128)S(1)}, f32[4,16,640]{2,0,1:T(4,128)S(1)}, u32[]{:S(2)}, u32[]{:S(2)}) %collective-permute-start.5) | collective-permute-done | bytes 163872 | tf_op jit(solution)/shard_map/ppermute | solution.py:190
  44.6 0.1 copy.58
  44.7 0.1 copy.56
  44.9 0.1 copy.60
  45.0 0.1 copy.57
  45.0 0.1 copy.61
  45.1 0.1 copy.59
  45.2 0.1 fusion.3
  45.4 1.8 %collective-permute-start.6 = (f32[2,16,640]{2,0,1:T(2,128)S(1)}, f32[2,16,640]{2,0,1:T(2,128)S(1)}, u32[]{:S(2)}, u32[]{:S(2)}) collective-permute-start(f32[2,16,640]{2,0,1:T(2,128)S(1)} %slice.85), channel_id=1, source_target_pairs={{0,4},{1,5},{2,6},{3,7},{4,0},{5,1},{6,2},{7,3},{8,12},{9,13},{10,... | collective-permute-start | bytes 245768 | tf_op jit(solution)/shard_map/ppermute | solution.py:190
  47.2 2.7 %collective-permute-done.6 = f32[2,16,640]{2,0,1:T(2,128)S(1)} collective-permute-done((f32[2,16,640]{2,0,1:T(2,128)S(1)}, f32[2,16,640]{2,0,1:T(2,128)S(1)}, u32[]{:S(2)}, u32[]{:S(2)}) %collective-permute-start.6) | collective-permute-done | bytes 81952 | tf_op jit(solution)/shard_map/ppermute | solution.py:190
  49.9 0.1 copy.64
  50.0 0.1 copy.62
  50.1 0.1 copy.66
  50.2 0.1 copy.63
  50.3 0.1 copy.67
  50.4 0.1 copy.65
  50.5 0.1 fusion.5
  50.7 2.8 %collective-permute-start.7 = (f32[1,16,640]{2,0,1:T(1,128)S(1)}, f32[1,16,640]{2,0,1:T(1,128)S(1)}, u32[]{:S(2)}, u32[]{:S(2)}) collective-permute-start(f32[1,16,640]{2,0,1:T(1,128)S(1)} %slice.89), channel_id=1, source_target_pairs={{0,8},{1,9},{2,10},{3,11},{4,12},{5,13},{6,14},{7,15},{8,0},{9,1},... | collective-permute-start | bytes 122888 | tf_op jit(solution)/shard_map/ppermute | solution.py:190
  53.5 2.2 %collective-permute-done.7 = f32[1,16,640]{2,0,1:T(1,128)S(1)} collective-permute-done((f32[1,16,640]{2,0,1:T(1,128)S(1)}, f32[1,16,640]{2,0,1:T(1,128)S(1)}, u32[]{:S(2)}, u32[]{:S(2)}) %collective-permute-start.7) | collective-permute-done | bytes 40992 | tf_op jit(solution)/shard_map/ppermute | solution.py:190
  55.6 0.2 fusion.9
  55.8 0.1 broadcast_select_fusion
  56.0 0.3 slice_reduce_fusion
  56.3 0.1 fusion.8
  56.4 0.6 %copy.68 = bf16[16,1,512]{2,0,1:T(8,128)(2,1)} copy(bf16[16,1,512]{2,1,0:T(2,128)(2,1)S(1)} %fusion.8) | data formatting | bytes 32768 | tf_op jit(solution)/shard_map/convert_element_type | solution.py:202
  (13 shorter events, 0.3 us)
Async XLA Ops:
  0.0 6.0 %collective-permute-start = (bf16[1,16,576]{2,1,0:T(8,128)(2,1)}, bf16[1,16,576]{2,1,0:T(8,128)(2,1)S(1)}, u32[]{:S(2)}, u32[]{:S(2)}) collective-permute-start(bf16[1,16,576]{2,1,0:T(8,128)(2,1)} %bitcast.31), channel_id=1, source_target_pairs={{0,8},{1,9},{2,10},{3,11},{4,12},{5,13},{6,14},{7,15},{8,0},{9,1},... | collective-permute-start | bytes 55304 | tf_op jit(solution)/shard_map/ppermute | solution.py:190
  6.8 4.1 %collective-permute-start.1 = (bf16[2,16,576]{2,1,0:T(8,128)(2,1)S(1)}, bf16[2,16,576]{2,1,0:T(8,128)(2,1)S(1)}, u32[]{:S(2)}, u32[]{:S(2)}) collective-permute-start(bf16[2,16,576]{2,1,0:T(8,128)(2,1)S(1)} %pad_maximum_fusion.2), channel_id=1, source_target_pairs={{0,4},{1,5},{2,6},{3,7},{4,0},{5,1},{6,2},{7,3},{8,12},{9,13},{10,... | collective-permute-start | bytes 110600 | tf_op jit(solution)/shard_map/ppermute | solution.py:190
  11.6 4.5 %collective-permute-start.2 = (bf16[4,16,576]{2,1,0:T(8,128)(2,1)S(1)}, bf16[4,16,576]{2,1,0:T(8,128)(2,1)S(1)}, u32[]{:S(2)}, u32[]{:S(2)}) collective-permute-start(bf16[4,16,576]{2,1,0:T(8,128)(2,1)S(1)} %pad_maximum_fusion.1), channel_id=1, source_target_pairs={{0,2},{1,3},{2,0},{3,1},{4,6},{5,7},{6,4},{7,5},{8,10},{9,11},{10,... | collective-permute-start | bytes 221192 | tf_op jit(solution)/shard_map/ppermute | solution.py:190
  16.9 1.5 %collective-permute-start.3 = (bf16[8,16,576]{2,1,0:T(8,128)(2,1)S(1)}, bf16[8,16,576]{2,1,0:T(8,128)(2,1)S(1)}, u32[]{:S(2)}, u32[]{:S(2)}) collective-permute-start(bf16[8,16,576]{2,1,0:T(8,128)(2,1)S(1)} %pad_maximum_fusion), channel_id=1, source_target_pairs={{0,1},{1,0},{2,3},{3,2},{4,5},{5,4},{6,7},{7,6},{8,9},{9,8},{10,11... | collective-permute-start | bytes 442376 | tf_op jit(solution)/shard_map/ppermute | solution.py:190
  33.9 1.7 %collective-permute-start.4 = (f32[8,16,640]{2,0,1:T(8,128)S(1)}, f32[8,16,640]{2,0,1:T(8,128)S(1)}, u32[]{:S(2)}, u32[]{:S(2)}) collective-permute-start(f32[8,16,640]{2,0,1:T(8,128)S(1)} %slice.77), channel_id=1, source_target_pairs={{0,1},{1,0},{2,3},{3,2},{4,5},{5,4},{6,7},{7,6},{8,9},{9,8},{10,11... | collective-permute-start | bytes 983048 | tf_op jit(solution)/shard_map/ppermute | solution.py:190
  38.1 6.5 %collective-permute-start.5 = (f32[4,16,640]{2,0,1:T(4,128)S(1)}, f32[4,16,640]{2,0,1:T(4,128)S(1)}, u32[]{:S(2)}, u32[]{:S(2)}) collective-permute-start(f32[4,16,640]{2,0,1:T(4,128)S(1)} %slice.81), channel_id=1, source_target_pairs={{0,2},{1,3},{2,0},{3,1},{4,6},{5,7},{6,4},{7,5},{8,10},{9,11},{10,... | collective-permute-start | bytes 491528 | tf_op jit(solution)/shard_map/ppermute | solution.py:190
  45.4 4.5 %collective-permute-start.6 = (f32[2,16,640]{2,0,1:T(2,128)S(1)}, f32[2,16,640]{2,0,1:T(2,128)S(1)}, u32[]{:S(2)}, u32[]{:S(2)}) collective-permute-start(f32[2,16,640]{2,0,1:T(2,128)S(1)} %slice.85), channel_id=1, source_target_pairs={{0,4},{1,5},{2,6},{3,7},{4,0},{5,1},{6,2},{7,3},{8,12},{9,13},{10,... | collective-permute-start | bytes 245768 | tf_op jit(solution)/shard_map/ppermute | solution.py:190
  50.7 5.0 %collective-permute-start.7 = (f32[1,16,640]{2,0,1:T(1,128)S(1)}, f32[1,16,640]{2,0,1:T(1,128)S(1)}, u32[]{:S(2)}, u32[]{:S(2)}) collective-permute-start(f32[1,16,640]{2,0,1:T(1,128)S(1)} %slice.89), channel_id=1, source_target_pairs={{0,8},{1,9},{2,10},{3,11},{4,12},{5,13},{6,14},{7,15},{8,0},{9,1},... | collective-permute-start | bytes 122888 | tf_op jit(solution)/shard_map/ppermute | solution.py:190

commit v2 on v0

v2 whole, which is shorter than its diff:
```python
import functools
import math

import jax
import jax.numpy as jnp
from jax import lax
from jax.experimental import pallas as pl
from jax.experimental.pallas import tpu as pltpu
from jax.sharding import PartitionSpec as P

ROPE = 64
LANES = 128
NEG = -1e30
NARROW = 1
CHUNK = 32

SOFTMAX_SCALE = (0.1 * math.log(40.0) + 1.0) ** 2 / math.sqrt(192.0)

VMEM = pl.BlockSpec(memory_space=pltpu.VMEM)
SMEM = pl.BlockSpec(memory_space=pltpu.SMEM)
HBM = pl.BlockSpec(memory_space=pltpu.HBM)


def in_hbm(x):
    return pltpu.with_memory_space_constraint(x, pltpu.HBM)


def plan_kernel(
    tokens, lengths_hbm, table_hbm, picks_hbm, own_hbm, owner_ref, count_ref, tiles_ref, own_ref,
    lengths_ref, table_ref, picks_ref, sems,
):
    copies = [
        pltpu.make_async_copy(src, dst, sems.at[i])
        for i, (src, dst) in enumerate(
            [(picks_hbm, picks_ref), (table_hbm, table_ref), (lengths_hbm, lengths_ref), (own_hbm, own_ref)]
        )
    ]
    for copy in copies:
        copy.start()
    slots, _, width = owner_ref.shape
    reqs, blocks = table_ref.shape
    picks = picks_ref.shape[1]
    pool = slots * width
    first_page = lax.axis_index("head") * pool
    block_lane = lax.broadcasted_iota(jnp.int32, (picks, blocks), 1)
    pool_lane = lax.broadcasted_iota(jnp.int32, (picks, pool), 1)
    owner = jnp.zeros((picks, pool), jnp.float32)
    count = jnp.zeros((picks, pool), jnp.float32)
    for copy in copies[:3]:
        copy.wait()
    by_row = picks_ref[...].astype(jnp.float32).T.astype(jnp.int32)
    for r in range(reqs):
        pick = by_row[:, r : r + 1]
        row = table_ref[r : r + 1, :].astype(jnp.float32)
        page = jnp.sum(
            jnp.where(block_lane == pick, row, 0.0), axis=1, keepdims=True
        ).astype(jnp.int32)
        live = jnp.clip(lengths_ref[r] - pick * tokens, 0, tokens)
        hit = pool_lane == page - first_page
        owner = jnp.where(hit, float(r + 1), owner)
        count = jnp.where(hit, live.astype(jnp.float32), count)
    owner = jnp.sum(owner, axis=0, keepdims=True)
    count = jnp.sum(count, axis=0, keepdims=True).astype(jnp.int32)
    used = jnp.int32(0)
    for tile in range(slots):
        own = owner[:, tile * width : (tile + 1) * width]
        needed = jnp.max(own) > 0.5
        slot = used

        @pl.when(needed)
        def _(tile=tile, own=own, slot=slot):
            tiles_ref[1 + slot] = tile
            owner_ref[slot] = own.astype(jnp.int32) - 1
            count_ref[slot] = count[:, tile * width : (tile + 1) * width]

        used = used + needed.astype(jnp.int32)
    tiles_ref[0] = used
    copies[3].wait()


def plan(lengths, page_table, selected, queries, slots, width, tokens):
    return pl.pallas_call(
        functools.partial(plan_kernel, tokens),
        out_shape=(
            pltpu.VMEM((slots, 1, width), jnp.int32),
            pltpu.VMEM((slots, 1, width), jnp.int32),
            pltpu.SMEM((slots + 1,), jnp.int32),
            pltpu.VMEM(queries.shape, queries.dtype),
        ),
        in_specs=[HBM] * 4,
        out_specs=(VMEM, VMEM, SMEM, VMEM),
        scratch_shapes=[
            pltpu.SMEM(lengths.shape, jnp.int32),
            pltpu.VMEM(page_table.shape, jnp.int32),
            pltpu.VMEM(selected.shape, jnp.int32),
            pltpu.SemaphoreType.DMA((4,)),
        ],
        compiler_params=pltpu.CompilerParams(vmem_limit_bytes=2**21),
        name="plan",
    )(in_hbm(lengths), in_hbm(page_table), in_hbm(selected), in_hbm(queries))


def tile_copy(tiles_ref, pool_ref, pages_ref, sem, slot, first, tokens):
    width = pages_ref.shape[2]
    part = pool_ref.at[pl.ds(first, tokens)]
    if pool_ref.shape[2] > width:
        lane = pl.multiple_of(tiles_ref[1 + slot] * width, width)
        part = part.at[:, :, pl.ds(lane, width)]
    return pltpu.make_async_copy(part, pages_ref.at[pl.ds(first, tokens)], sem)


def fetch_kernel(first, tokens, tiles_ref, pool_ref, *refs):
    pages_ref, sem = refs[-2:]

    @pl.when(tiles_ref[0] > 0)
    def _():
        copy = tile_copy(tiles_ref, pool_ref, pages_ref, sem, 0, first, tokens)
        copy.start()
        copy.wait()


def fetch(tiles, pool, width, first, tokens, pages=None):
    more = [] if pages is None else [pages]
    return pl.pallas_call(
        functools.partial(fetch_kernel, first, tokens),
        out_shape=pltpu.VMEM((*pool.shape[:2], width), jnp.bfloat16),
        in_specs=[SMEM, HBM] + [VMEM] * len(more),
        out_specs=VMEM,
        scratch_shapes=[pltpu.SemaphoreType.DMA],
        input_output_aliases={2: 0} if more else {},
        compiler_params=pltpu.CompilerParams(vmem_limit_bytes=2**20),
        name=f"fetch{first}",
    )(tiles, pool, *more)


def by_request(owner_ref, values_ref, used, reqs, join, empty):
    def step(slot, joined):
        own, values = owner_ref[slot], values_ref[slot]
        return tuple(join(x, jnp.where(own == r, values, empty)) for r, x in enumerate(joined))

    start = jnp.full(values_ref.shape[1:], empty, jnp.float32)
    return lax.fori_loop(0, used, step, (start,) * reqs)


def attend_kernel(
    sizes, tiles_ref, owner_ref, count_ref, queries_ref, pool_ref, _, pages_ref, keep_ref, send_ref,
    scores, tops, sums, numer, sem,
):
    reqs, heads, latent, chunk = sizes
    tokens, channels, width = pages_ref.shape
    group = 2 if width == LANES else 1
    used = tiles_ref[0]

    def reload(slot):
        copy = tile_copy(tiles_ref, pool_ref, pages_ref, sem, slot, 0, tokens)
        copy.start()
        copy.wait()

    @pl.loop(0, used)
    def _(slot):
        @pl.when(slot > 0)
        def _():
            reload(slot)

        own, live = owner_ref[slot], count_ref[slot]
        own_wide = jnp.concatenate([own] * group, axis=1)
        tops[slot] = jnp.full((heads, width), NEG, jnp.float32)

        @pl.loop(0, tokens // chunk)
        def _(part):
            top = tops[slot]
            for t in range(0, chunk, group):
                token = part * chunk + t
                both = jnp.dot(
                    queries_ref[...],
                    jnp.concatenate([pages_ref[token + g] for g in range(group)], axis=1),
                    preferred_element_type=jnp.float32,
                )
                mine = both[:heads]
                for r in range(1, reqs):
                    mine = jnp.where(own_wide == r, both[r * heads : (r + 1) * heads], mine)
                for g in range(group):
                    score = mine[:, g * width : (g + 1) * width] * SOFTMAX_SCALE
                    score = jnp.where(live > token + g, score, NEG)
                    scores[slot, token + g] = score
                    top = jnp.maximum(top, score)
            tops[slot] = top

    row_top = [jnp.max(x, axis=1, keepdims=True) for x in by_request(owner_ref, tops, used, reqs, jnp.maximum, NEG)]
    numer[...] = jnp.zeros(numer.shape, jnp.float32)

    @pl.loop(0, used)
    def _(step):
        slot = used - 1 - step

        @pl.when(step > 0)
        def _():
            reload(slot)

        own, live = owner_ref[slot], count_ref[slot]
        shift = jnp.zeros((heads, width), jnp.float32)
        for r in range(reqs):
            shift = jnp.where(own == r, row_top[r], shift)
        sums[slot] = jnp.zeros((heads, width), jnp.float32)

        @pl.loop(0, tokens // chunk)
        def _(part):
            acc = sums[slot]
            weights, values = [], []
            for t in range(chunk):
                token = part * chunk + t
                weight = jnp.where(live > token, jnp.exp(scores[slot, token] - shift), 0.0)
                acc = acc + weight
                spread = [jnp.where(own == r, weight, 0.0).astype(jnp.bfloat16) for r in range(reqs)]
                weights.append(jnp.concatenate(spread, axis=0))
                values.append(pages_ref[token, :latent])
            sums[slot] = acc
            numer[...] += lax.dot_general(
                jnp.concatenate(weights, axis=1),
                jnp.concatenate(values, axis=1),
                (((1,), (1,)), ((), ())),
                preferred_element_type=jnp.float32,
            )

    cut = heads // 2
    totals = by_request(owner_ref, sums, used, reqs, jnp.add, 0.0)
    for r in range(reqs):
        total = jnp.sum(totals[r], axis=1, keepdims=True)
        last = tail_of(row_top[r], total, jnp.float32)
        for ref, first in ((keep_ref, 0), (send_ref, cut)):
            rows = pl.ds(r, cut, stride=reqs)
            mine = numer[r * heads + first : r * heads + first + cut]
            for i in range(latent // LANES):
                ref.at[i][rows, :] = mine[:, i * LANES : (i + 1) * LANES]
            ref.at[latent // LANES][rows, :] = last[first : first + cut]


def attend(queries, pages, pool, owner, count, tiles):
    reqs, heads, channels = queries.shape
    slots = owner.shape[0]
    tokens, _, width = pages.shape
    latent = channels - ROPE
    chunk = math.gcd(CHUNK, tokens)
    rows = reqs * heads
    half = pltpu.VMEM((latent // LANES + 1, rows // 2, LANES), jnp.float32)
    _, keep, send = pl.pallas_call(
        functools.partial(attend_kernel, (reqs, heads, latent, chunk)),
        out_shape=(pltpu.VMEM(pages.shape, pages.dtype), half, half),
        in_specs=[SMEM] + [VMEM] * 3 + [HBM, VMEM],
        out_specs=(VMEM,) * 3,
        scratch_shapes=[
            pltpu.VMEM((slots, tokens, heads, width), jnp.float32),
            pltpu.VMEM((slots, heads, width), jnp.float32),
            pltpu.VMEM((slots, heads, width), jnp.float32),
            pltpu.VMEM((rows, latent), jnp.float32),
            pltpu.SemaphoreType.DMA,
        ],
        input_output_aliases={5: 0},
        compiler_params=pltpu.CompilerParams(vmem_limit_bytes=(24 if heads > 16 else 12) * 2**20),
        name="attend",
    )(tiles, owner, count, queries.reshape(rows, channels), pool, pages)
    return keep, send


def tail_of(top, total, dtype):
    lane = lax.broadcasted_iota(jnp.int32, (*top.shape[:-1], LANES), top.ndim - 1)
    tail = jnp.zeros(lane.shape, jnp.float32)
    terms = []
    for value in (top, total):
        for _ in range(1 if dtype == jnp.float32 else 3):
            term = value.astype(dtype).astype(jnp.float32)
            terms.append(term)
            value = value - term
    for i, term in enumerate(terms):
        tail = jnp.where(lane == i, term, tail)
    return tail.astype(dtype)


def split_tail(tail):
    wide = tail.astype(jnp.float32)
    count = 1 if tail.dtype == jnp.float32 else 3
    parts = [wide[..., i : i + 1] for i in range(2 * count)]
    return sum(parts[1:count], parts[0]), sum(parts[count + 1 :], parts[count])


def combine(mine_ref, theirs_ref, rows):
    mine_top, mine_total = split_tail(mine_ref[mine_ref.shape[0] - 1, rows])
    their_top, their_total = split_tail(theirs_ref[theirs_ref.shape[0] - 1, rows])
    top = jnp.maximum(mine_top, their_top)
    mine_scale, their_scale = jnp.exp(mine_top - top), jnp.exp(their_top - top)
    numer = [
        mine_ref[i, rows] * mine_scale + theirs_ref[i, rows].astype(jnp.float32) * their_scale
        for i in range(mine_ref.shape[0] - 1)
    ]
    return numer, top, mine_total * mine_scale + their_total * their_scale


def merge_kernel(mine_ref, theirs_ref, keep_ref, send_ref):
    cut = keep_ref.shape[1]
    for rows, ref in ((pl.ds(cut, cut), send_ref), (pl.ds(0, cut), keep_ref)):
        numer, top, total = combine(mine_ref, theirs_ref, rows)
        for i, value in enumerate(numer):
            ref[i] = value.astype(ref.dtype)
        ref[len(numer)] = tail_of(top, total, ref.dtype)


def finish_kernel(mine_ref, theirs_ref, out_ref):
    numer, _, total = combine(mine_ref, theirs_ref, slice(None))
    for i, value in enumerate(numer):
        out_ref[:, i * LANES : (i + 1) * LANES] = (value / total).astype(out_ref.dtype)


def merge(mine, theirs, wire):
    tiles, rows, _ = mine.shape
    half = (tiles, rows // 2, LANES)
    return pl.pallas_call(
        merge_kernel,
        out_shape=(pltpu.VMEM(half, jnp.float32), pltpu.VMEM(half, wire)),
        in_specs=[VMEM, VMEM],
        out_specs=(VMEM, VMEM),
        compiler_params=pltpu.CompilerParams(vmem_limit_bytes=2**21),
        name=f"merge{rows}",
    )(mine, theirs)


def finish(mine, theirs):
    tiles, rows, _ = mine.shape
    return pl.pallas_call(
        finish_kernel,
        out_shape=jax.ShapeDtypeStruct((rows, (tiles - 1) * LANES), jnp.bfloat16),
        in_specs=[VMEM, VMEM],
        out_specs=VMEM,
        compiler_params=pltpu.CompilerParams(vmem_limit_bytes=2**20),
        name="finish",
    )(mine, theirs)


def local(queries, kv_pages, page_table, lengths, selected):
    pages_dev, tokens = kv_pages.shape[:2]
    devices = lax.axis_size("head")
    strides = [1 << b for b in reversed(range(devices.bit_length() - 1))]
    width = LANES if pages_dev % LANES == 0 else pages_dev
    slots = pages_dev // width

    def swap(x, stride):
        return lax.ppermute(x, "head", [(i, i ^ stride) for i in range(devices)])

    pool = in_hbm(kv_pages.transpose(1, 2, 0))
    asked = queries.transpose(1, 0, 2)
    owner, count, tiles, own = plan(lengths, page_table, selected, asked, slots, width, tokens)
    gathered = jnp.concatenate([own, swap(asked, strides[0])], axis=0)
    pages, first = None, 0
    for stride in strides[1:]:
        gathered = lax.optimization_barrier(gathered)
        arriving = swap(gathered, stride)
        if first < tokens:
            pages = fetch(tiles, pool, width, first, tokens // 2, pages)
            first += tokens // 2
            gathered, pages = lax.optimization_barrier((gathered, pages))
        gathered = jnp.concatenate([gathered, arriving], axis=0)
    keep, send = attend(gathered.transpose(1, 0, 2), pages, pool, owner, count, tiles)
    for i, stride in enumerate(reversed(strides[1:])):
        keep, send = merge(keep, swap(send, stride), jnp.bfloat16 if i < NARROW else jnp.float32)
    return finish(keep, swap(send, strides[0]))[:, None, :]


def solution(mesh):
    return jax.shard_map(
        local,
        mesh=mesh,
        in_specs=(
            P("grp", "head", None),
            P(("grp", "head"), None, None),
            P("grp", None),
            P("grp"),
            P("grp", None),
        ),
        out_specs=P("grp", "head", None),
        check_vma=False,
    )
```

time: 232 us -> 41.1 us (0.18)
  blocking collectives: 84.1 us -> 0 us
  local copies, waits for them, and re-layouts: 81.5 us -> 0.06 us
  other arithmetic: 16.7 us -> 0.11 us
  Pallas kernels: 0 us -> 15.6 us
  between operations: 13.6 us -> 0.08 us
  starting transfers between devices: 0.01 us -> 13 us
  matrix products: 12.6 us -> 0 us
  waiting for transfers between devices: 21.9 us -> 12.1 us
    unnamed x12 -> x0, local copies, waits for them, and re-layouts: 55.7 us -> none
    unnamed x1 -> x0, blocking collectives: 30.1 us -> none
    pmax x1 -> x0, blocking collectives: 30 us -> none  [local(): row_top = lax.pmax(local_top, 'head')]
    gather x10 -> x0, local copies, waits for them, and re-layouts: 24.2 us -> none  [the longest x1 12.2 us: local(): blocks = kv_pages[local_page]]
    all_gather x1 -> x0, blocking collectives: 24 us -> none  [local(): all_queries = lax.all_gather(queries, 'head', axis=1, tiled=True)]
    reduce_scatter x1 -> x0, waiting for transfers between devices: 21.8 us -> none  [local(): lax.psum_scatter(numer_sum, 'head', scatter_dimension=1, tiled=True)]
    pallas_call x0 -> x8, Pallas kernels: none -> 15.6 us  [the longest x1 6.75 us: attend(): pl.pallas_call(functools.partial(attend_kernel, (reqs, heads, latent, chu...]
    ppermute x0 -> x8, starting transfers between devices: none -> 13 us  [swap(): return lax.ppermute(x, 'head', [(i, i ^ stride) for i in range(devices)])]
  transfers between devices with their start and end apart: 1 -> 8, of which waited for: 1 -> 7; matrix products, arithmetic and copies ran while one was open for 1% -> 0% of each run, Pallas kernels for 0% -> 18%
where the time goes in v2:
time: 41.1 us; the launch traced here: 40.9 us
  Pallas kernels  15.6 us (38%)
  starting transfers between devices  13 us (32%)
  waiting for transfers between devices  12.1 us (29%)
    ppermute x8, starting transfers between devices, swap(): return lax.ppermute(x, 'head', [(i, i ^ stride) for i in range(devices)])  13 us
    ppermute x8, waiting for transfers between devices, swap(): return lax.ppermute(x, 'head', [(i, i ^ stride) for i in range(devices)])  12.1 us
    pallas_call x1, Pallas kernels, attend(): pl.pallas_call(functools.partial(attend_kernel, (reqs, heads, latent, chu...  6.75 us
    pallas_call x2, Pallas kernels, fetch(): pl.pallas_call(functools.partial(fetch_kernel, first, tokens), out_shape=...  4.69 us
    pallas_call x1, Pallas kernels, plan(): pl.pallas_call(functools.partial(plan_kernel, tokens), out_shape=(pltpu.V...  2.69 us
  transfers between devices with their start and end apart: 8, of which 7 were waited for; matrix products, arithmetic and copies ran while one was open for 0% of the time, Pallas kernels for 18%

profile of v2, /device:TPU:0, one launch (start us, length us, event | category | flops | bytes accessed | tf_op | source)
XLA Modules:
  0.0 40.9 jit_solution(6824507309133432562)
XLA Ops:
  0.0 4.1 %collective-permute-start = (bf16[1,16,576]{2,1,0:T(8,128)(2,1)}, bf16[1,16,576]{2,1,0:T(8,128)(2,1)S(1)}, u32[]{:S(2)}, u32[]{:S(2)}) collective-permute-start(bf16[1,16,576]{2,1,0:T(8,128)(2,1)} %bitcast.10), channel_id=1, source_target_pairs={{0,8},{1,9},{2,10},{3,11},{4,12},{5,13},{6,14},{7,15},{8,0},{9,1},... | collective-permute-start | bytes 55304 | tf_op jit(solution)/shard_map/ppermute | solution.py:346
  4.1 2.7 %plan.1 = (s32[4,1,128]{2,1,0:T(1,128)S(1)}, s32[4,1,128]{2,1,0:T(1,128)S(1)}, s32[5]{0:T(128)S(4)}, bf16[1,16,576]{2,1,0:T(8,128)(2,1)S(1)}) custom-call(s32[16]{0:T(128)} %lengths_hbm.1, s32[16,512]{1,0:T(8,128)} %table_hbm.1, s32[16,32]{1,0:T(8,128)} %picks_hbm.1, bf16[1,16,576]{2,1,0:T(8,128)(2,1)} %bitcast.11), custom_call_target="tpu_custom_call" | custom-call | tf_op jit(solution)/shard_map/plan/pallas_call | solution.py:82
  6.8 0.0 collective-permute-done
  6.8 1.6 %collective-permute-start.1 = (bf16[2,16,576]{2,1,0:T(8,128)(2,1)S(1)}, bf16[2,16,576]{2,1,0:T(8,128)(2,1)S(1)}, u32[]{:S(2)}, u32[]{:S(2)}) collective-permute-start(bf16[2,16,576]{2,1,0:T(8,128)(2,1)S(1)} %pad_maximum_fusion.2), channel_id=1, source_target_pairs={{0,4},{1,5},{2,6},{3,7},{4,0},{5,1},{6,2},{7,3},{8,12},{9,13},{10,... | collective-permute-start | bytes 110600 | tf_op jit(solution)/shard_map/ppermute | solution.py:346
  8.4 2.3 %fetch0.1.refs_0_ = bf16[64,576,128]{2,1,0:T(8,128)(2,1)S(1)} custom-call(s32[5]{0:T(128)S(4)} %get-tuple-element.21.tiles_ref, bf16[64,576,512]{2,1,0:T(8,128)(2,1)} %bitcast.7), custom_call_target="tpu_custom_call" | custom-call | tf_op jit(solution)/shard_map/fetch0/pallas_call | solution.py:124
  10.8 0.1 collective-permute-done.1
  10.9 1.6 %collective-permute-start.2 = (bf16[4,16,576]{2,1,0:T(8,128)(2,1)S(1)}, bf16[4,16,576]{2,1,0:T(8,128)(2,1)S(1)}, u32[]{:S(2)}, u32[]{:S(2)}) collective-permute-start(bf16[4,16,576]{2,1,0:T(8,128)(2,1)S(1)} %pad_maximum_fusion.1), channel_id=1, source_target_pairs={{0,2},{1,3},{2,0},{3,1},{4,6},{5,7},{6,4},{7,5},{8,10},{9,11},{10,... | collective-permute-start | bytes 221192 | tf_op jit(solution)/shard_map/ppermute | solution.py:346
  12.4 2.3 %fetch32.1._ = bf16[64,576,128]{2,1,0:T(8,128)(2,1)S(1)} custom-call(s32[5]{0:T(128)S(4)} %get-tuple-element.21.tiles_ref, bf16[64,576,512]{2,1,0:T(8,128)(2,1)} %bitcast.8, bf16[64,576,128]{2,1,0:T(8,128)(2,1)S(1)} %fetch0.1.refs_0_), custom_call_target="tpu_custom_call", output_to_operand_aliasing={{}: (2, {})} | custom-call | tf_op jit(solution)/shard_map/fetch32/pallas_call | solution.py:124
  14.8 0.6 %collective-permute-done.2 = bf16[4,16,576]{2,1,0:T(8,128)(2,1)S(1)} collective-permute-done((bf16[4,16,576]{2,1,0:T(8,128)(2,1)S(1)}, bf16[4,16,576]{2,1,0:T(8,128)(2,1)S(1)}, u32[]{:S(2)}, u32[]{:S(2)}) %collective-permute-start.2) | collective-permute-done | bytes 73760 | tf_op jit(solution)/shard_map/ppermute | solution.py:346
  15.4 0.1 collective-permute-start.3
  15.5 1.4 %collective-permute-done.3 = bf16[8,16,576]{2,1,0:T(8,128)(2,1)S(1)} collective-permute-done((bf16[8,16,576]{2,1,0:T(8,128)(2,1)S(1)}, bf16[8,16,576]{2,1,0:T(8,128)(2,1)S(1)}, u32[]{:S(2)}, u32[]{:S(2)}) %collective-permute-start.3) | collective-permute-done | bytes 147488 | tf_op jit(solution)/shard_map/ppermute | solution.py:346
  16.9 0.1 copy.8
  17.0 6.8 %attend.1 = (bf16[64,576,128]{2,1,0:T(8,128)(2,1)S(1)}, f32[5,128,128]{2,1,0:T(8,128)S(1)}, f32[5,128,128]{2,1,0:T(8,128)S(1)}) custom-call(s32[5]{0:T(128)S(4)} %get-tuple-element.21.tiles_ref, s32[4,1,128]{2,1,0:T(1,128)S(1)} %get-tuple-element.22.owner_ref, s32[4,1,128]{2,1,0:T(1,128)S(1)} %get-tuple-element.23.count_ref, ...), custom_call_target="tpu_custom_call", output_to_operand_aliasing={{0}: (5, {})} | custom-call | tf_op jit(solution)/shard_map/attend/pallas_call | solution.py:246
  23.8 0.2 collective-permute-start.4
  24.0 1.5 %collective-permute-done.4.theirs_ref = f32[5,128,128]{2,1,0:T(8,128)S(1)} collective-permute-done((f32[5,128,128]{2,1,0:T(8,128)S(1)}, f32[5,128,128]{2,1,0:T(8,128)S(1)}, u32[]{:S(2)}, u32[]{:S(2)}) %collective-permute-start.4) | collective-permute-done | bytes 327712 | tf_op jit(solution)/shard_map/ppermute | solution.py:346
  25.5 0.2 merge128.1
  25.7 1.6 %collective-permute-start.5 = (bf16[5,64,128]{2,1,0:T(8,128)(2,1)S(1)}, bf16[5,64,128]{2,1,0:T(8,128)(2,1)S(1)}, u32[]{:S(2)}, u32[]{:S(2)}) collective-permute-start(bf16[5,64,128]{2,1,0:T(8,128)(2,1)S(1)} %get-tuple-element.32), channel_id=1, source_target_pairs={{0,2},{1,3},{2,0},{3,1},{4,6},{5,7},{6,4},{7,5},{8,10},{9,11},{10,... | collective-permute-start | bytes 245768 | tf_op jit(solution)/shard_map/ppermute | solution.py:346
  27.2 3.0 %collective-permute-done.5.theirs_ref = bf16[5,64,128]{2,1,0:T(8,128)(2,1)S(1)} collective-permute-done((bf16[5,64,128]{2,1,0:T(8,128)(2,1)S(1)}, bf16[5,64,128]{2,1,0:T(8,128)(2,1)S(1)}, u32[]{:S(2)}, u32[]{:S(2)}) %collective-permute-start.5) | collective-permute-done | bytes 81952 | tf_op jit(solution)/shard_map/ppermute | solution.py:346
  30.2 0.3 merge64.1
  30.5 1.6 %collective-permute-start.6 = (f32[5,32,128]{2,1,0:T(8,128)S(1)}, f32[5,32,128]{2,1,0:T(8,128)S(1)}, u32[]{:S(2)}, u32[]{:S(2)}) collective-permute-start(f32[5,32,128]{2,1,0:T(8,128)S(1)} %get-tuple-element.34), channel_id=1, source_target_pairs={{0,4},{1,5},{2,6},{3,7},{4,0},{5,1},{6,2},{7,3},{8,12},{9,13},{10,... | collective-permute-start | bytes 245768 | tf_op jit(solution)/shard_map/ppermute | solution.py:346
  32.2 2.9 %collective-permute-done.6.theirs_ref = f32[5,32,128]{2,1,0:T(8,128)S(1)} collective-permute-done((f32[5,32,128]{2,1,0:T(8,128)S(1)}, f32[5,32,128]{2,1,0:T(8,128)S(1)}, u32[]{:S(2)}, u32[]{:S(2)}) %collective-permute-start.6) | collective-permute-done | bytes 81952 | tf_op jit(solution)/shard_map/ppermute | solution.py:346
  35.0 0.2 merge32.1
  35.2 2.2 %collective-permute-start.7 = (f32[5,16,128]{2,1,0:T(8,128)S(1)}, f32[5,16,128]{2,1,0:T(8,128)S(1)}, u32[]{:S(2)}, u32[]{:S(2)}) collective-permute-start(f32[5,16,128]{2,1,0:T(8,128)S(1)} %get-tuple-element.36), channel_id=1, source_target_pairs={{0,8},{1,9},{2,10},{3,11},{4,12},{5,13},{6,14},{7,15},{8,0},{9,1},... | collective-permute-start | bytes 122888 | tf_op jit(solution)/shard_map/ppermute | solution.py:346
  37.4 2.7 %collective-permute-done.7.theirs_ref = f32[5,16,128]{2,1,0:T(8,128)S(1)} collective-permute-done((f32[5,16,128]{2,1,0:T(8,128)S(1)}, f32[5,16,128]{2,1,0:T(8,128)S(1)}, u32[]{:S(2)}, u32[]{:S(2)}) %collective-permute-start.7) | collective-permute-done | bytes 40992 | tf_op jit(solution)/shard_map/ppermute | solution.py:346
  40.1 0.8 %finish.1 = bf16[16,512]{1,0:T(8,128)(2,1)} custom-call(f32[5,16,128]{2,1,0:T(8,128)S(1)} %get-tuple-element.35.mine_ref, f32[5,16,128]{2,1,0:T(8,128)S(1)} %collective-permute-done.7.theirs_ref), custom_call_target="tpu_custom_call" | custom-call | tf_op jit(solution)/shard_map/finish/pallas_call | solution.py:328
  (4 shorter events, 0.1 us)
Async XLA Ops:
  0.0 6.8 %collective-permute-start = (bf16[1,16,576]{2,1,0:T(8,128)(2,1)}, bf16[1,16,576]{2,1,0:T(8,128)(2,1)S(1)}, u32[]{:S(2)}, u32[]{:S(2)}) collective-permute-start(bf16[1,16,576]{2,1,0:T(8,128)(2,1)} %bitcast.10), channel_id=1, source_target_pairs={{0,8},{1,9},{2,10},{3,11},{4,12},{5,13},{6,14},{7,15},{8,0},{9,1},... | collective-permute-start | bytes 55304 | tf_op jit(solution)/shard_map/ppermute | solution.py:346
  6.8 4.1 %collective-permute-start.1 = (bf16[2,16,576]{2,1,0:T(8,128)(2,1)S(1)}, bf16[2,16,576]{2,1,0:T(8,128)(2,1)S(1)}, u32[]{:S(2)}, u32[]{:S(2)}) collective-permute-start(bf16[2,16,576]{2,1,0:T(8,128)(2,1)S(1)} %pad_maximum_fusion.2), channel_id=1, source_target_pairs={{0,4},{1,5},{2,6},{3,7},{4,0},{5,1},{6,2},{7,3},{8,12},{9,13},{10,... | collective-permute-start | bytes 110600 | tf_op jit(solution)/shard_map/ppermute | solution.py:346
  10.9 4.5 %collective-permute-start.2 = (bf16[4,16,576]{2,1,0:T(8,128)(2,1)S(1)}, bf16[4,16,576]{2,1,0:T(8,128)(2,1)S(1)}, u32[]{:S(2)}, u32[]{:S(2)}) collective-permute-start(bf16[4,16,576]{2,1,0:T(8,128)(2,1)S(1)} %pad_maximum_fusion.1), channel_id=1, source_target_pairs={{0,2},{1,3},{2,0},{3,1},{4,6},{5,7},{6,4},{7,5},{8,10},{9,11},{10,... | collective-permute-start | bytes 221192 | tf_op jit(solution)/shard_map/ppermute | solution.py:346
  15.4 1.5 %collective-permute-start.3 = (bf16[8,16,576]{2,1,0:T(8,128)(2,1)S(1)}, bf16[8,16,576]{2,1,0:T(8,128)(2,1)S(1)}, u32[]{:S(2)}, u32[]{:S(2)}) collective-permute-start(bf16[8,16,576]{2,1,0:T(8,128)(2,1)S(1)} %pad_maximum_fusion), channel_id=1, source_target_pairs={{0,1},{1,0},{2,3},{3,2},{4,5},{5,4},{6,7},{7,6},{8,9},{9,8},{10,11... | collective-permute-start | bytes 442376 | tf_op jit(solution)/shard_map/ppermute | solution.py:346
  23.8 1.7 %collective-permute-start.4 = (f32[5,128,128]{2,1,0:T(8,128)S(1)}, f32[5,128,128]{2,1,0:T(8,128)S(1)}, u32[]{:S(2)}, u32[]{:S(2)}) collective-permute-start(f32[5,128,128]{2,1,0:T(8,128)S(1)} %get-tuple-element.30), channel_id=1, source_target_pairs={{0,1},{1,0},{2,3},{3,2},{4,5},{5,4},{6,7},{7,6},{8,9},{9,8},{10,11... | collective-permute-start | bytes 983048 | tf_op jit(solution)/shard_map/ppermute | solution.py:346
  25.7 4.6 %collective-permute-start.5 = (bf16[5,64,128]{2,1,0:T(8,128)(2,1)S(1)}, bf16[5,64,128]{2,1,0:T(8,128)(2,1)S(1)}, u32[]{:S(2)}, u32[]{:S(2)}) collective-permute-start(bf16[5,64,128]{2,1,0:T(8,128)(2,1)S(1)} %get-tuple-element.32), channel_id=1, source_target_pairs={{0,2},{1,3},{2,0},{3,1},{4,6},{5,7},{6,4},{7,5},{8,10},{9,11},{10,... | collective-permute-start | bytes 245768 | tf_op jit(solution)/shard_map/ppermute | solution.py:346
  30.5 4.5 %collective-permute-start.6 = (f32[5,32,128]{2,1,0:T(8,128)S(1)}, f32[5,32,128]{2,1,0:T(8,128)S(1)}, u32[]{:S(2)}, u32[]{:S(2)}) collective-permute-start(f32[5,32,128]{2,1,0:T(8,128)S(1)} %get-tuple-element.34), channel_id=1, source_target_pairs={{0,4},{1,5},{2,6},{3,7},{4,0},{5,1},{6,2},{7,3},{8,12},{9,13},{10,... | collective-permute-start | bytes 245768 | tf_op jit(solution)/shard_map/ppermute | solution.py:346
  35.2 4.9 %collective-permute-start.7 = (f32[5,16,128]{2,1,0:T(8,128)S(1)}, f32[5,16,128]{2,1,0:T(8,128)S(1)}, u32[]{:S(2)}, u32[]{:S(2)}) collective-permute-start(f32[5,16,128]{2,1,0:T(8,128)S(1)} %get-tuple-element.36), channel_id=1, source_target_pairs={{0,8},{1,9},{2,10},{3,11},{4,12},{5,13},{6,14},{7,15},{8,0},{9,1},... | collective-permute-start | bytes 122888 | tf_op jit(solution)/shard_map/ppermute | solution.py:346
